TPU v7x, 32 devices: a whole 2x2x4 slice. The times are simulated.
32 devices in a mesh: ex: 4 (over z), col: 4 (over y, core), lay: 2 (over x).
Axes of the slice: x: 2, y: 2, z: 4, core: 2. Of those that a mesh axis runs over, the one named last changes fastest.
Arguments:
- normalized: bfloat16 [256, 2, 4, 3584], P('ex', 'lay', None, 'col'), may hold values from -6 to 6
- upstream: bfloat16 [256, 2, 4, 3584], P('ex', 'lay', None, 'col'), may hold values from -3 to 3
- owner_order: int32 [4, 64], P('ex'), may hold values from 0 to 63, each once within a row
- sketch_index: int32 [2, 28, 4], P(None, 'col'), may hold values from 0 to 63, all different within a row
- sketch_scale: bfloat16 [2, 28, 4], P(None, 'col'), may hold values from -1.5 to 1.5
- query_sketch: bfloat16 [4, 8192], P('ex', 'col'), may hold values from -0.0625 to 0.0625
Outputs:
- sketch: bfloat16 [256, 8192], P(('ex', 'lay'), 'col')
- scores: float32 [256, 4], P(('ex', 'lay'), 'col')
Inputs may be any that keep to these rules, and one draw needn't show every extreme that they name: Each row is an ordering of the 64 examples of one block; the example at place j of row g is training example g * 64 + owner_order[g, j]. `sketch_index`: the 4 output blocks of one input block are distinct; every output block is named by some input block.
All inputs are finite; a program needn't handle non-finite values.
Results may differ from a plain program's by a relative error of at most 0.0049.
Values may be sent and summed in bfloat16 or wider, within the bound.
A program may use at most 64 MiB of HBM per device.

v0:
```python
import functools
import math

import jax
import jax.numpy as jnp
from jax import lax
from jax.experimental import pallas as pl
from jax.experimental.pallas import tpu as pltpu
from jax.sharding import PartitionSpec as P

MESH = pl.DeviceIdType.MESH
LANES = 128
CHUNKS = 4


def signs():
    bits = lax.broadcasted_iota(jnp.int32, (LANES, LANES), 0) & lax.broadcasted_iota(
        jnp.int32, (LANES, LANES), 1
    )
    bits = bits ^ (bits >> 4)
    bits = bits ^ (bits >> 2)
    bits = bits ^ (bits >> 1)
    return (1 - 2 * (bits & 1)).astype(jnp.float32).astype(jnp.bfloat16)


def kernel(
    sizes,
    x_hbm,
    u_hbm,
    order_hbm,
    index_hbm,
    scale_hbm,
    query_hbm,
    sketch_ref,
    scores_ref,
    order_ref,
    index_ref,
    scale_ref,
    query_ref,
    x_ref,
    u_ref,
    grads_ref,
    owned_ref,
    pieces_ref,
    own_tab_ref,
    tabs_ref,
    own_query_f32_ref,
    own_query_ref,
    queries_ref,
    had_ref,
    splat_ref,
    turned_tab_ref,
    weights_ref,
    rot_ref,
    total_ref,
    in_sem,
    small_sem,
    piece_send,
    piece_recv,
    relay_send,
    tab_send,
    tab_recv,
    query_send,
    query_recv,
    ready_sem,
):
    n_ex, n_col, n_lay, per_col, k_sel = sizes
    ex, col, lay = lax.axis_index("ex"), lax.axis_index("col"), lax.axis_index("lay")
    examples, tokens, features = x_ref.shape
    rows = examples // n_lay
    in_blocks = features // LANES
    layers = index_ref.shape[0]
    out_blocks = query_ref.shape[1] // LANES
    padded = weights_ref.shape[2]
    chunk = examples // CHUNKS
    sibling = col + 1 - 2 * lax.rem(col, 2)
    scale = 1.0 / math.sqrt(float(LANES))

    loads = []
    for i in range(CHUNKS):
        part = pl.ds(i * chunk, chunk)
        pair = [
            pltpu.make_async_copy(x_hbm.at[part], x_ref.at[part], in_sem.at[2 * i]),
            pltpu.make_async_copy(u_hbm.at[part], u_ref.at[part], in_sem.at[2 * i + 1]),
        ]
        for copy in pair:
            copy.start()
        loads.append(pair)

    smalls = [
        pltpu.make_async_copy(source, held, small_sem.at[i])
        for i, (source, held) in enumerate(
            [
                (query_hbm, query_ref),
                (index_hbm, index_ref),
                (scale_hbm, scale_ref),
                (order_hbm, order_ref),
            ]
        )
    ]
    for copy in smalls:
        copy.start()

    barrier = pltpu.get_barrier_semaphore()
    for dl in range(n_lay):
        for dc in range(n_col):
            if dl or dc:
                pl.semaphore_signal(
                    barrier,
                    inc=1,
                    device_id={
                        "ex": ex,
                        "col": lax.rem(col + dc, n_col),
                        "lay": lax.rem(lay + dl, n_lay),
                    },
                    device_id_type=MESH,
                )
    has_lower, has_upper = ex > 0, ex < n_ex - 1

    def signal_plane(sem, step):
        pl.semaphore_signal(
            sem,
            inc=1,
            device_id={"ex": ex + step, "col": col, "lay": lay},
            device_id_type=MESH,
        )

    pl.when(has_lower)(lambda: signal_plane(barrier, -1))
    pl.when(has_upper)(lambda: signal_plane(barrier, 1))

    had_ref[...] = signs()
    for copy in smalls:
        copy.wait()
    own_tab_ref[...] = jnp.full(own_tab_ref.shape, -1.0, jnp.float32)
    for layer in range(layers):
        own_tab_ref[layer, 0:k_sel, 0:in_blocks] = index_ref[layer].astype(jnp.float32)
        own_tab_ref[layer, k_sel : 2 * k_sel, 0:in_blocks] = scale_ref[layer].astype(jnp.float32)
    for o in range(out_blocks):
        own_query_f32_ref[o : o + 1, :] = query_ref[:, o * LANES : (o + 1) * LANES].astype(
            jnp.float32
        )
    own_query_ref[...] = own_query_f32_ref[...].astype(jnp.bfloat16)

    def tab_copy(dc):
        return pltpu.make_async_remote_copy(
            src_ref=own_tab_ref,
            dst_ref=tabs_ref.at[col],
            send_sem=tab_send.at[dc],
            recv_sem=tab_recv.at[col],
            device_id={"ex": ex, "col": lax.rem(col + dc, n_col), "lay": lay},
            device_id_type=MESH,
        )

    for i in range(CHUNKS):
        if i == CHUNKS // 2:
            planes = has_lower.astype(jnp.int32) + has_upper.astype(jnp.int32)
            pl.semaphore_wait(barrier, n_lay * n_col - 1 + planes)
            pl.when(jnp.logical_not(has_lower))(lambda: signal_plane(ready_sem.at[0], 1))
            pl.when(jnp.logical_not(has_upper))(lambda: signal_plane(ready_sem.at[1], -1))
            tab_copies = [tab_copy(dc) for dc in range(1, n_col)]
            for copy in tab_copies:
                copy.start()

        for copy in loads[i]:
            copy.wait()
        part = slice(i * chunk, (i + 1) * chunk)
        grads_ref[part, :] = jnp.sum(
            x_ref[part].astype(jnp.float32) * u_ref[part].astype(jnp.float32), axis=1
        ).astype(jnp.bfloat16)
    chosen = (
        lax.broadcasted_iota(jnp.int32, (examples, examples), 0) == order_ref[...]
    ).astype(jnp.float32)
    chosen = chosen.T.astype(jnp.bfloat16)
    ordered = jnp.dot(chosen, grads_ref[...], preferred_element_type=jnp.float32)
    for owner in range(n_lay):
        owned_ref[owner] = ordered[owner * rows : (owner + 1) * rows].astype(jnp.bfloat16)

    asker = ex // per_col
    slot = lax.rem(ex, per_col)

    def query_copy(target):
        return pltpu.make_async_remote_copy(
            src_ref=own_query_ref,
            dst_ref=queries_ref.at[slot, col],
            send_sem=query_send.at[target],
            recv_sem=query_recv.at[slot, col],
            device_id={"ex": target, "col": asker, "lay": lay},
            device_id_type=MESH,
        )

    def keep_query():
        return pltpu.make_async_copy(
            own_query_ref, queries_ref.at[slot, col], query_recv.at[slot, col]
        )

    def send_query(target, wanted):
        mine = jnp.logical_and(target == ex, asker == col)

        @pl.when(jnp.logical_and(wanted, jnp.logical_not(mine)))
        def _():
            query_copy(target).start()

        @pl.when(jnp.logical_and(wanted, mine))
        def _():
            keep_query().start()

    def lower_planes():
        @pl.when(has_lower)
        def _():
            pl.semaphore_wait(ready_sem.at[0], 1)
            pl.when(has_upper)(lambda: signal_plane(ready_sem.at[0], 1))

        for target in range(n_ex):
            send_query(target, target <= ex)

    def upper_planes(here):
        @pl.when(jnp.logical_and(here, has_upper))
        def _():
            pl.semaphore_wait(ready_sem.at[1], 1)
            pl.when(has_lower)(lambda: signal_plane(ready_sem.at[1], -1))

        for target in range(n_ex):
            send_query(target, jnp.logical_and(here, target > ex))

    offsets = [
        (dl, dc) for dl in range(n_lay) for dc in range(0, n_col, 2) if dl or dc
    ]
    offsets.sort(key=lambda at: (at[0] != 0) + (at[1] != 0))

    def piece_copy(number, dl, dc):
        to_lay, to_col = lax.rem(lay + dl, n_lay), lax.rem(col + dc, n_col)
        return pltpu.make_async_remote_copy(
            src_ref=owned_ref.at[to_lay],
            dst_ref=pieces_ref.at[lay, col],
            send_sem=piece_send.at[number],
            recv_sem=piece_recv.at[lay, col],
            device_id={"ex": ex, "col": to_col, "lay": to_lay},
            device_id_type=MESH,
        )

    def relay_copy(number, source, at_lay, at_col):
        return pltpu.make_async_remote_copy(
            src_ref=source,
            dst_ref=pieces_ref.at[at_lay, at_col],
            send_sem=relay_send.at[number],
            recv_sem=piece_recv.at[at_lay, at_col],
            device_id={"ex": ex, "col": sibling, "lay": lay},
            device_id_type=MESH,
        )

    def arrive(at_lay, at_col):
        pltpu.make_async_remote_copy(
            src_ref=owned_ref.at[0],
            dst_ref=pieces_ref.at[at_lay, at_col],
            send_sem=relay_send.at[0],
            recv_sem=piece_recv.at[at_lay, at_col],
            device_id={"ex": ex, "col": sibling, "lay": lay},
            device_id_type=MESH,
        ).wait_recv()

    sends = [piece_copy(n, dl, dc) for n, (dl, dc) in enumerate(offsets)]
    for copy in reversed(sends):
        copy.start()
    own_relay = relay_copy(len(offsets), owned_ref.at[lay], lay, col)
    own_relay.start()
    sends.append(own_relay)

    lower_planes()
    upper_planes(has_lower)

    tabs_ref[col] = own_tab_ref[...]
    for dc in range(1, n_col):
        source = lax.rem(col + dc, n_col)
        pltpu.make_async_remote_copy(
            src_ref=own_tab_ref,
            dst_ref=tabs_ref.at[source],
            send_sem=tab_send.at[dc],
            recv_sem=tab_recv.at[source],
            device_id={"ex": ex, "col": source, "lay": lay},
            device_id_type=MESH,
        ).wait_recv()

    def table(at_lay, at_col, first, count):
        targets = (first + lax.broadcasted_iota(jnp.int32, (count, LANES), 0)).astype(jnp.float32)
        value = jnp.zeros((count, LANES), jnp.float32)
        for k in range(k_sel):
            index = tabs_ref[at_col, at_lay, k : k + 1, :]
            gain = tabs_ref[at_col, at_lay, k_sel + k : k_sel + k + 1, :]
            value = value + jnp.where(targets == index, gain, 0.0)
        return value

    for at_lay in range(layers):
        for at_col in range(n_col):
            mine = table(at_lay, at_col, col * out_blocks, out_blocks) * scale
            for b in range(in_blocks):
                splat_ref[at_lay, at_col, b] = jnp.broadcast_to(
                    mine[:, b : b + 1], (out_blocks, LANES)
                )

    def rotate(source, at_lay, at_col):
        piece = source[...]
        stacked = jnp.concatenate(
            [piece[:, b * LANES : (b + 1) * LANES] for b in range(in_blocks)], axis=0
        )
        rot_ref[at_lay, at_col] = jnp.dot(
            stacked, had_ref[...], preferred_element_type=jnp.float32
        ).reshape(in_blocks, rows, LANES)

    group = 4

    def combine(at_lay, at_col, first, last):
        for o in range(0, out_blocks, group):
            if first:
                sums = [jnp.zeros((rows, LANES), jnp.float32) for _ in range(group)]
            else:
                sums = [total_ref[o + g] for g in range(group)]
            for b in range(in_blocks):
                turned = rot_ref[at_lay, at_col, b]
                for g in range(group):
                    sums[g] = sums[g] + turned * splat_ref[at_lay, at_col, b, o + g : o + g + 1, :]
            for g in range(group):
                if last:
                    sketch_ref[:, (o + g) * LANES : (o + g + 1) * LANES] = sums[g].astype(
                        jnp.bfloat16
                    )
                else:
                    total_ref[o + g] = sums[g]

    rotate(owned_ref.at[lay], lay, col)
    combine(lay, col, True, False)

    for at_lay in range(layers):
        for at_col in range(n_col):
            whole = table(at_lay, at_col, 0, n_col * out_blocks).T
            turned_tab_ref[at_lay, at_col] = whole[0:padded].astype(jnp.bfloat16)

    arrive(lay, sibling)
    rotate(pieces_ref.at[lay, sibling], lay, sibling)
    combine(lay, sibling, False, False)
    upper_planes(jnp.logical_not(has_lower))
    relays = []
    for number, (dl, dc) in enumerate(offsets):
        at_lay, at_col = lax.rem(lay + dl, n_lay), lax.rem(col + dc, n_col)
        arrive(at_lay, at_col)
        relay = relay_copy(number, pieces_ref.at[at_lay, at_col], at_lay, at_col)
        relay.start()
        relays.append(relay)
        rotate(pieces_ref.at[at_lay, at_col], at_lay, at_col)
        combine(at_lay, at_col, False, False)
    for number, (dl, dc) in enumerate(offsets):
        at_lay, at_col = lax.rem(lay + dl, n_lay), lax.rem(sibling + dc, n_col)
        last = number == len(offsets) - 1
        arrive(at_lay, at_col)
        rotate(pieces_ref.at[at_lay, at_col], at_lay, at_col)
        combine(at_lay, at_col, False, last)

    for j in range(per_col):
        holder = col * per_col + j
        for other in range(n_col):
            here = jnp.logical_and(holder == ex, other == col)

            @pl.when(jnp.logical_not(here))
            def _():
                pltpu.make_async_remote_copy(
                    src_ref=own_query_ref,
                    dst_ref=queries_ref.at[j, other],
                    send_sem=query_send.at[0],
                    recv_sem=query_recv.at[j, other],
                    device_id={"ex": holder, "col": other, "lay": lay},
                    device_id_type=MESH,
                ).wait_recv()

            @pl.when(here)
            def _():
                keep_query().wait()

    asked = jnp.concatenate(
        [
            queries_ref[j].astype(jnp.float32).reshape(n_col * out_blocks, LANES)
            for j in range(per_col)
        ],
        axis=1,
    ).astype(jnp.bfloat16)
    weights_ref[...] = jnp.dot(
        turned_tab_ref[...].reshape(layers * n_col * padded, n_col * out_blocks),
        asked,
        preferred_element_type=jnp.float32,
    ).reshape(weights_ref.shape)
    for q in range(per_col):
        sums = jnp.zeros((rows, LANES), jnp.float32)
        for at_lay in range(layers):
            for at_col in range(n_col):
                for b in range(in_blocks):
                    sums = sums + rot_ref[at_lay, at_col, b] * weights_ref[
                        at_lay, at_col, b : b + 1, q * LANES : (q + 1) * LANES
                    ]
        scores_ref[q : q + 1, :] = jnp.sum(sums.T, axis=0, keepdims=True) * scale

    for copy in sends + relays + tab_copies:
        copy.wait_send()
    for target in range(n_ex):
        mine = jnp.logical_and(target == ex, asker == col)

        @pl.when(jnp.logical_not(mine))
        def _():
            query_copy(target).wait_send()


def solution(mesh):
    n_ex, n_col, n_lay = (mesh.shape[name] for name in ("ex", "col", "lay"))

    def local(normalized, upstream, owner_order, sketch_index, sketch_scale, query_sketch):
        examples, own_layers, tokens, features = normalized.shape
        assert own_layers == 1
        layers, in_blocks, k_sel = sketch_index.shape
        width = query_sketch.shape[1]
        out_blocks = width // LANES
        per_col = n_ex * query_sketch.shape[0] // n_col
        rows = examples // n_lay
        padded = -(-in_blocks // 16) * 16
        vmem = pl.BlockSpec(memory_space=pltpu.VMEM)
        dma = pltpu.SemaphoreType.DMA
        sketch, scores = pl.pallas_call(
            functools.partial(kernel, (n_ex, n_col, n_lay, per_col, k_sel)),
            out_shape=(
                pltpu.VMEM((rows, width), jnp.bfloat16),
                pltpu.VMEM((per_col, rows), jnp.float32),
            ),
            in_specs=[pl.BlockSpec(memory_space=pl.ANY)] * 6,
            out_specs=(vmem, vmem),
            scratch_shapes=[
                pltpu.VMEM(owner_order.shape, jnp.int32),
                pltpu.VMEM((layers, k_sel, in_blocks), jnp.int32),
                pltpu.VMEM((layers, k_sel, in_blocks), jnp.bfloat16),
                pltpu.VMEM(query_sketch.shape, jnp.bfloat16),
                pltpu.VMEM((examples, tokens, features), jnp.bfloat16),
                pltpu.VMEM((examples, tokens, features), jnp.bfloat16),
                pltpu.VMEM((examples, features), jnp.bfloat16),
                pltpu.VMEM((n_lay, rows, features), jnp.bfloat16),
                pltpu.VMEM((n_lay, n_col, rows, features), jnp.bfloat16),
                pltpu.VMEM((layers, 2 * k_sel, LANES), jnp.float32),
                pltpu.VMEM((n_col, layers, 2 * k_sel, LANES), jnp.float32),
                pltpu.VMEM((out_blocks, LANES), jnp.float32),
                pltpu.VMEM((out_blocks, LANES), jnp.bfloat16),
                pltpu.VMEM((per_col, n_col, out_blocks, LANES), jnp.bfloat16),
                pltpu.VMEM((LANES, LANES), jnp.bfloat16),
                pltpu.VMEM((layers, n_col, in_blocks, out_blocks, LANES), jnp.float32),
                pltpu.VMEM((layers, n_col, padded, n_col * out_blocks), jnp.bfloat16),
                pltpu.VMEM((layers, n_col, padded, per_col * LANES), jnp.float32),
                pltpu.VMEM((n_lay, n_col, in_blocks, rows, LANES), jnp.float32),
                pltpu.VMEM((out_blocks, rows, LANES), jnp.float32),
                dma((2 * CHUNKS,)),
                dma((4,)),
                dma((n_lay * n_col,)),
                dma((n_lay, n_col)),
                dma((n_lay * n_col,)),
                dma((n_col,)),
                dma((n_col,)),
                dma((n_ex,)),
                dma((per_col, n_col)),
                pltpu.SemaphoreType.REGULAR((2,)),
            ],
            compiler_params=pltpu.CompilerParams(collective_id=0, has_side_effects=True),
        )(
            normalized.reshape(examples, tokens, features),
            upstream.reshape(examples, tokens, features),
            owner_order,
            jnp.swapaxes(sketch_index, 1, 2),
            jnp.swapaxes(sketch_scale, 1, 2),
            query_sketch,
        )
        return sketch, scores.T

    placed = (
        P("ex", "lay", None, "col"),
        P("ex", "lay", None, "col"),
        P("ex", None),
        P(None, "col", None),
        P(None, "col", None),
        P("ex", "col"),
    )
    return jax.shard_map(
        local,
        mesh=mesh,
        in_specs=placed,
        out_specs=(P(("ex", "lay"), "col"), P(("ex", "lay"), "col")),
        check_vma=False,
    )
```

profile of v0, /device:TPU:0, one launch (start us, length us, event | category | flops | bytes accessed | tf_op | source)
XLA Modules:
  0.0 13.2 jit_solution(13419250567807446645)
XLA Ops:
  0.6 11.4 %shard_map.77 = (bf16[32,2048]{1,0:T(8,128)(2,1)S(1)}, f32[1,32]{1,0:T(1,128)S(1)}) custom-call(bf16[64,4,896]{2,1,0:T(4,128)(2,1)} %bitcast.6, bf16[64,4,896]{2,1,0:T(4,128)(2,1)} %bitcast.7, s32[1,64]{1,0:T(1,128)} %order_hbm.1, s32[2,4,7]{2,1,0:T(4,128)} %bitcast.8, bf16[2,4,7]{2,1,0:T(4,128)(2,1)} %bitcast.9, bf16[1,2048]{1,0:T(2,128)(2,1)} %query_hbm.1), custom_call_target="tpu_custom_call" | custom-call | tf_op jit(solution)/shard_map/pallas_call | solution.py:423
  12.0 0.7 %copy.10 = bf16[32,2048]{1,0:T(8,128)(2,1)} copy(bf16[32,2048]{1,0:T(8,128)(2,1)S(1)} %get-tuple-element.6) | data formatting | bytes 262144
  12.7 0.5 %copy.11 = f32[32,1]{0,1:T(1,128)} copy(f32[32,1]{0,1:T(1,128)S(1)} %bitcast.5) | data formatting | bytes 256
where the time goes:
time: 13.3 us; the launch traced here: 13.2 us
  Pallas kernels  11.4 us (86%)
  local copies, waits for them, and re-layouts  1.17 us (9%)
  between operations  0.64 us (5%)
    pallas_call x1, Pallas kernels, local(): pl.pallas_call(functools.partial(kernel, (n_ex, n_col, n_lay, per_col, k_...  11.4 us
    unnamed x2, local copies, waits for them, and re-layouts  1.17 us

commit v1 on v0

v1 whole, which is shorter than its diff:
```python
import functools
import math

import jax
import jax.numpy as jnp
from jax import lax
from jax.experimental import pallas as pl
from jax.experimental.pallas import tpu as pltpu
from jax.sharding import PartitionSpec as P

MESH = pl.DeviceIdType.MESH
LANES = 128
WAVES = 4
GROUP = 4
TILE = 16


def cuts(total):
    waves = min(WAVES, total)
    sizes = [total // waves + (i < total % waves) for i in range(waves)]
    return [(sum(sizes[:i]), sizes[i]) for i in range(waves)]


def signs():
    bits = lax.broadcasted_iota(jnp.int32, (LANES, LANES), 0) & lax.broadcasted_iota(
        jnp.int32, (LANES, LANES), 1
    )
    bits = bits ^ (bits >> 4)
    bits = bits ^ (bits >> 2)
    bits = bits ^ (bits >> 1)
    return (1 - 2 * (bits & 1)).astype(jnp.float32).astype(jnp.bfloat16)


def kernel(
    sizes,
    x_hbm,
    u_hbm,
    order_hbm,
    index_hbm,
    scale_hbm,
    query_hbm,
    sketch_ref,
    scores_ref,
    order_ref,
    index_ref,
    scale_ref,
    query_ref,
    xu_ref,
    owned_ref,
    arrived_ref,
    sibling_ref,
    own_tab_ref,
    tabs_ref,
    own_query_f32_ref,
    own_query_ref,
    queries_ref,
    had_ref,
    splat_ref,
    turned_tab_ref,
    weights_ref,
    rot_ref,
    total_ref,
    score_ref,
    load_sem,
    small_sem,
    send_sem,
    wave_sem,
    sibling_sem,
    tab_sem,
    query_sem,
    ready_sem,
):
    n_ex, n_col, n_lay, per_col, k_sel = sizes
    ex, col, lay = lax.axis_index("ex"), lax.axis_index("col"), lax.axis_index("lay")
    examples, tokens, features = x_hbm.shape
    pack = TILE // tokens
    rows = examples // n_lay
    in_blocks = features // LANES
    layers = index_ref.shape[0]
    stride = LANES // layers
    out_blocks = query_ref.shape[1] // LANES
    half = n_col // 2
    others = n_lay * half - 1
    core, chip = lax.rem(col, 2), lay * half + col // 2
    sibling = col + 1 - 2 * core
    scale = 1.0 / math.sqrt(float(LANES))
    waves = cuts(in_blocks)

    load_parts = [pl.ds(0, waves[0][1] * LANES)]
    if len(waves) > 1:
        load_parts.append(pl.ds(waves[1][0] * LANES, features - waves[1][0] * LANES))
    smalls = [
        pltpu.make_async_copy(source, held, small_sem.at[i])
        for i, (source, held) in enumerate(
            [
                (order_hbm, order_ref),
                (index_hbm, index_ref),
                (scale_hbm, scale_ref),
                (query_hbm, query_ref),
            ]
        )
    ]
    smalls[0].start()
    for k, part in enumerate(load_parts):
        for i, source in enumerate((x_hbm, u_hbm)):
            split = source.reshape(examples // pack, pack, tokens, features)
            for r in range(pack):
                pltpu.make_async_copy(
                    split.at[:, r, :, part],
                    xu_ref.at[i, :, pl.ds(r * tokens, tokens), part],
                    load_sem.at[k],
                ).start()
        if k == 0:
            for copy in smalls[1:]:
                copy.start()

    barrier = pltpu.get_barrier_semaphore()
    asker = ex // per_col
    asked_first = col * per_col

    def greet(sem, at_ex, at_col, at_lay):
        pl.semaphore_signal(
            sem,
            inc=1,
            device_id={"ex": at_ex, "col": at_col, "lay": at_lay},
            device_id_type=MESH,
        )

    for dl in reversed(range(n_lay)):
        for dc in reversed(range(n_col)):
            if dl or dc:
                greet(barrier, ex, lax.rem(col + dc, n_col), lax.rem(lay + dl, n_lay))

    def greet_askers(at_ex, carry):
        greet(barrier, at_ex, asker, lay)
        return carry

    def greet_sources(sem):
        def body(at_ex, carry):
            for at_col in range(n_col):
                greet(sem, at_ex, at_col, lay)
            return carry

        return body

    lax.fori_loop(ex + 1, n_ex, greet_askers, 0)
    lax.fori_loop(
        jnp.maximum(ex + 1, asked_first), asked_first + per_col, greet_sources(barrier), 0
    )
    below = jnp.clip(ex - asked_first, 0, per_col)
    greetings = n_lay * n_col - 1 + ex + n_col * below

    had_ref[...] = signs()
    own_tab_ref[...] = jnp.full(own_tab_ref.shape, -1.0, jnp.float32)

    def turn(stacked):
        return jnp.dot(stacked, had_ref[...], preferred_element_type=jnp.float32)

    def wave_part(k):
        first, count = waves[k]
        return pl.ds(2 * others * first, 2 * others * count)

    def piece_copy(k, number):
        first, count = waves[k]
        target = number + (chip <= number).astype(jnp.int32)
        slot = chip - (chip > target).astype(jnp.int32)
        to_lay = target // half
        return pltpu.make_async_remote_copy(
            src_ref=owned_ref.at[to_lay, pl.ds(first, count)],
            dst_ref=arrived_ref.at[
                pl.ds(2 * others * first + (2 * slot + core) * count, count)
            ],
            send_sem=send_sem.at[0],
            recv_sem=wave_sem.at[k],
            device_id={"ex": ex, "col": 2 * lax.rem(target, half) + 1, "lay": to_lay},
            device_id_type=MESH,
        )

    def to_sibling(source, target, send, recv):
        return pltpu.make_async_remote_copy(
            src_ref=source,
            dst_ref=target,
            send_sem=send,
            recv_sem=recv,
            device_id={"ex": ex, "col": sibling, "lay": lay},
            device_id_type=MESH,
        )

    def own_copy(first, count):
        part = pl.ds(first, count)
        return to_sibling(
            owned_ref.at[lay, part], sibling_ref.at[part], send_sem.at[1], sibling_sem.at[0]
        )

    def relay_copy(k):
        part = arrived_ref.at[wave_part(k)]
        return to_sibling(part, part, send_sem.at[2], wave_sem.at[k])

    def tab_copy(dc):
        return pltpu.make_async_remote_copy(
            src_ref=tabs_ref.at[0],
            dst_ref=tabs_ref.at[dc],
            send_sem=tab_sem.at[0],
            recv_sem=tab_sem.at[1],
            device_id={"ex": ex, "col": lax.rem(col + dc, n_col), "lay": lay},
            device_id_type=MESH,
        )

    def all_tabs():
        part = tabs_ref.at[pl.ds(1, n_col - 1)]
        return to_sibling(part, part, tab_sem.at[0], tab_sem.at[1])

    smalls[0].wait()
    chosen = (
        lax.broadcasted_iota(jnp.int32, (examples * tokens, examples), 0) // tokens
        == order_ref[...]
    ).astype(jnp.float32)
    chosen = chosen.T.astype(jnp.bfloat16)
    for copy in smalls[1:]:
        copy.wait()
    for layer in range(layers):
        at = slice(stride * layer, stride * layer + in_blocks)
        own_tab_ref[0:k_sel, at] = index_ref[layer].astype(jnp.float32)
        own_tab_ref[k_sel : 2 * k_sel, at] = scale_ref[layer].astype(jnp.float32)
    tabs_ref[0] = own_tab_ref[...].astype(jnp.bfloat16)
    for o in range(out_blocks):
        own_query_f32_ref[o : o + 1, :] = query_ref[:, o * LANES : (o + 1) * LANES].astype(
            jnp.float32
        )
    own_query_ref[...] = own_query_f32_ref[...].astype(jnp.bfloat16)

    for k, (first, count) in enumerate(waves):
        if k < len(load_parts):
            part = load_parts[k]
            pltpu.make_async_copy(
                xu_ref.at[:, :, :, part], xu_ref.at[:, :, :, part], load_sem.at[k]
            ).wait()
        x, u = (
            xu_ref[i, :, :, first * LANES : (first + count) * LANES]
            .reshape(examples * tokens, count * LANES)
            .astype(jnp.float32)
            for i in range(2)
        )
        product = x * u
        high = product.astype(jnp.bfloat16)
        low = (product - high.astype(jnp.float32)).astype(jnp.bfloat16)
        ordered = (
            jnp.dot(chosen, high, preferred_element_type=jnp.float32)
            + jnp.dot(chosen, low, preferred_element_type=jnp.float32)
        ).astype(jnp.bfloat16)
        stacked = jnp.concatenate(
            [ordered[:, b * LANES : (b + 1) * LANES] for b in range(count)], axis=0
        )
        if k:
            stacked = turn(stacked).astype(jnp.bfloat16)
        for owner in range(n_lay):
            for b in range(count):
                at = b * examples + owner * rows
                owned_ref[owner, first + b] = stacked[at : at + rows]
        if k == 0:
            pl.semaphore_wait(barrier, greetings)
            lax.fori_loop(
                asked_first,
                jnp.minimum(asked_first + per_col, ex),
                greet_sources(ready_sem.at[0]),
                0,
            )
        if others:
            piece_copy(k, 0).start()
        if k == 0:
            for dc in range(1, n_col):
                tab_copy(dc).start()
        else:
            for number in range(1, others):
                piece_copy(k - 1, number).start()
        own_copy(first, count).start()
    for number in range(1, others):
        piece_copy(len(waves) - 1, number).start()

    place = lax.rem(ex, per_col) * n_col + col
    mine = asker == col

    def query_copy(target):
        return pltpu.make_async_remote_copy(
            src_ref=own_query_ref,
            dst_ref=queries_ref.at[place],
            send_sem=query_sem.at[0],
            recv_sem=query_sem.at[1],
            device_id={"ex": target, "col": asker, "lay": lay},
            device_id_type=MESH,
        )

    def send_query(target, carry):
        query_copy(target).start()
        return carry

    @pl.when(mine)
    def _():
        pltpu.make_async_copy(own_query_ref, queries_ref.at[place], query_sem.at[1]).start()

    pl.when(jnp.logical_not(mine))(lambda: query_copy(ex).start())
    lax.fori_loop(0, ex, send_query, 0)

    def queries_up():
        @pl.when(ex < n_ex - 1)
        def _():
            pl.semaphore_wait(ready_sem.at[0], n_ex - 1 - ex)
            lax.fori_loop(ex + 1, n_ex, send_query, 0)

    def slot_of(source):
        return lax.rem(col - source + n_col, n_col)

    def table(slot, first, count):
        tab = tabs_ref[slot].astype(jnp.float32)
        targets = (first + lax.broadcasted_iota(jnp.int32, (count, LANES), 0)).astype(jnp.float32)
        value = jnp.zeros((count, LANES), jnp.float32)
        for k in range(k_sel):
            value = value + jnp.where(
                targets == tab[k : k + 1, :], tab[k_sel + k : k_sel + k + 1, :], 0.0
            )
        return value

    def spread(slot):
        own = table(slot, col * out_blocks, out_blocks) * scale
        for at_lay in range(layers):
            for b in range(in_blocks):
                at = stride * at_lay + b
                splat_ref[at_lay, slot, b] = jnp.broadcast_to(
                    own[:, at : at + 1], (out_blocks, LANES)
                )

    metas = []

    def combine(source, blocks, turned, first=False, last=False):
        base, count = len(metas), len(blocks)
        metas.extend(blocks)
        if turned:
            rot_ref[base : base + count] = source.astype(jnp.float32)
        else:
            rot_ref[base : base + count] = turn(source.reshape(count * rows, LANES)).reshape(
                count, rows, LANES
            )
        for o in range(0, out_blocks, GROUP):
            if first:
                sums = [jnp.zeros((rows, LANES), jnp.float32) for _ in range(GROUP)]
            else:
                sums = [total_ref[o + g] for g in range(GROUP)]
            for i, (at_lay, slot, b) in enumerate(blocks):
                value = rot_ref[base + i]
                for g in range(GROUP):
                    sums[g] = sums[g] + value * splat_ref[at_lay, slot, b, o + g : o + g + 1, :]
            for g in range(GROUP):
                if last:
                    sketch_ref[:, (o + g) * LANES : (o + g + 1) * LANES] = sums[g].astype(
                        jnp.bfloat16
                    )
                else:
                    total_ref[o + g] = sums[g]

    def await_wave(k):
        part = arrived_ref.at[wave_part(k)]
        to_sibling(part, part, send_sem.at[2], wave_sem.at[k]).wait_recv()

    def combine_wave(k, last=False):
        first, count = waves[k]
        blocks = []
        for number in range(others):
            source = number + (chip <= number).astype(jnp.int32)
            for odd in range(2):
                slot = slot_of(2 * lax.rem(source, half) + odd)
                blocks += [(source // half, slot, first + b) for b in range(count)]
        low = 2 * others * first
        combine(arrived_ref[low : low + 2 * others * count], blocks, k > 0, last=last)
        add_scores(len(metas) - len(blocks), len(metas))

    early = waves[0][1]
    spread(0)
    combine(owned_ref[lay, :early], [(lay, 0, b) for b in range(early)], False, first=True)
    combine(owned_ref[lay, early:], [(lay, 0, b) for b in range(early, in_blocks)], True)

    all_tabs().wait_recv()
    for slot in range(1, n_col):
        spread(slot)
    to_sibling(sibling_ref, sibling_ref, send_sem.at[1], sibling_sem.at[0]).wait_recv()
    near = slot_of(sibling)
    combine(sibling_ref[:early], [(lay, near, b) for b in range(early)], False)
    combine(sibling_ref[early:], [(lay, near, b) for b in range(early, in_blocks)], True)
    for slot in range(n_col):
        whole = table(slot, 0, n_col * out_blocks).T
        turned_tab_ref[slot] = whole.astype(jnp.bfloat16)

    def add_scores(start, stop):
        for q in range(per_col):
            value = score_ref[q]
            for i in range(start, stop):
                at_lay, slot, b = metas[i]
                value = value + rot_ref[i] * weights_ref[
                    slot, at_lay, b : b + 1, q * LANES : (q + 1) * LANES
                ]
            score_ref[q] = value

    def start_scores(stop):
        pltpu.make_async_copy(queries_ref, queries_ref, query_sem.at[1]).wait()
        asked = jnp.concatenate(
            [
                queries_ref[j * n_col : (j + 1) * n_col]
                .astype(jnp.float32)
                .reshape(n_col * out_blocks, LANES)
                for j in range(per_col)
            ],
            axis=1,
        ).astype(jnp.bfloat16)
        weights_ref[...] = jnp.dot(
            turned_tab_ref[...].reshape(n_col * LANES, n_col * out_blocks),
            asked,
            preferred_element_type=jnp.float32,
        ).reshape(weights_ref.shape)
        score_ref[...] = jnp.zeros_like(score_ref)
        add_scores(0, stop)

    timely = jnp.logical_and(asked_first == ex, per_col == 1)

    @pl.when(timely)
    def _():
        start_scores(2 * in_blocks)

    @pl.when(jnp.logical_not(timely))
    def _():
        weights_ref[...] = jnp.zeros_like(weights_ref)
        score_ref[...] = jnp.zeros_like(score_ref)

    odd_core = core == 1
    pl.when(jnp.logical_not(odd_core))(queries_up)
    last = len(waves) - 1
    for k in range(len(waves)):
        await_wave(k)
        pl.when(odd_core)(lambda: relay_copy(k).start())
        combine_wave(k, last=k == last)
        if k == 0:
            pl.when(odd_core)(queries_up)

    pl.when(jnp.logical_not(timely))(lambda: start_scores(len(metas)))
    for q in range(per_col):
        scores_ref[q : q + 1, :] = jnp.sum(score_ref[q].T, axis=0, keepdims=True) * scale

    part = arrived_ref.at[pl.ds(0, others * in_blocks)]
    to_sibling(part, part, send_sem.at[0], wave_sem.at[0]).wait_send()
    to_sibling(sibling_ref, sibling_ref, send_sem.at[1], sibling_sem.at[0]).wait_send()
    all_tabs().wait_send()

    @pl.when(odd_core)
    def _():
        to_sibling(arrived_ref, arrived_ref, send_sem.at[2], wave_sem.at[0]).wait_send()

    def sent_queries(count):
        part = queries_ref.at[pl.ds(0, count)]
        to_sibling(part, part, query_sem.at[0], query_sem.at[1]).wait_send()

    pl.when(jnp.logical_not(mine))(lambda: sent_queries(n_ex))
    if n_ex > 1:
        pl.when(mine)(lambda: sent_queries(n_ex - 1))


def put_out(sketch_ref, scores_ref, sketch_hbm, scores_hbm, sem):
    copies = [
        pltpu.make_async_copy(sketch_ref, sketch_hbm, sem.at[0]),
        pltpu.make_async_copy(scores_ref, scores_hbm, sem.at[1]),
    ]
    for copy in copies:
        copy.start()
    for copy in copies:
        copy.wait()


def solution(mesh):
    n_ex, n_col, n_lay = (mesh.shape[name] for name in ("ex", "col", "lay"))

    def local(normalized, upstream, owner_order, sketch_index, sketch_scale, query_sketch):
        examples, own_layers, tokens, features = normalized.shape
        layers, in_blocks, k_sel = sketch_index.shape
        width = query_sketch.shape[1]
        out_blocks = width // LANES
        assert TILE % tokens == 0 and examples * tokens % TILE == 0
        assert own_layers == 1 and query_sketch.shape[0] == 1 and n_col % 2 == 0
        assert n_col * out_blocks <= 256 and in_blocks <= LANES // layers
        per_col = n_ex // n_col
        rows = examples // n_lay
        waves = len(cuts(in_blocks))
        others = n_lay * n_col // 2 - 1
        vmem = pl.BlockSpec(memory_space=pltpu.VMEM)
        hbm = pl.BlockSpec(memory_space=pl.ANY)
        dma = pltpu.SemaphoreType.DMA
        sketch, scores = pl.pallas_call(
            functools.partial(kernel, (n_ex, n_col, n_lay, per_col, k_sel)),
            out_shape=(
                pltpu.VMEM((rows, width), jnp.bfloat16),
                pltpu.VMEM((per_col, rows), jnp.float32),
            ),
            in_specs=[hbm] * 6,
            out_specs=(vmem, vmem),
            scratch_shapes=[
                pltpu.VMEM(owner_order.shape, jnp.int32),
                pltpu.VMEM((layers, k_sel, in_blocks), jnp.int32),
                pltpu.VMEM((layers, k_sel, in_blocks), jnp.bfloat16),
                pltpu.VMEM(query_sketch.shape, jnp.bfloat16),
                pltpu.VMEM((2, examples * tokens // TILE, TILE, features), jnp.bfloat16),
                pltpu.VMEM((n_lay, in_blocks, rows, LANES), jnp.bfloat16),
                pltpu.VMEM((2 * others * in_blocks, rows, LANES), jnp.bfloat16),
                pltpu.VMEM((in_blocks, rows, LANES), jnp.bfloat16),
                pltpu.VMEM((2 * k_sel, LANES), jnp.float32),
                pltpu.VMEM((n_col, 2 * k_sel, LANES), jnp.bfloat16),
                pltpu.VMEM((out_blocks, LANES), jnp.float32),
                pltpu.VMEM((out_blocks, LANES), jnp.bfloat16),
                pltpu.VMEM((n_ex, out_blocks, LANES), jnp.bfloat16),
                pltpu.VMEM((LANES, LANES), jnp.bfloat16),
                pltpu.VMEM((layers, n_col, in_blocks, out_blocks, LANES), jnp.float32),
                pltpu.VMEM((n_col, LANES, n_col * out_blocks), jnp.bfloat16),
                pltpu.VMEM((n_col, layers, LANES // layers, per_col * LANES), jnp.float32),
                pltpu.VMEM((n_lay * n_col * in_blocks, rows, LANES), jnp.float32),
                pltpu.VMEM((out_blocks, rows, LANES), jnp.float32),
                pltpu.VMEM((per_col, rows, LANES), jnp.float32),
                dma((min(waves, 2),)),
                dma((4,)),
                dma((3,)),
                dma((waves,)),
                dma((1,)),
                dma((2,)),
                dma((2,)),
                pltpu.SemaphoreType.REGULAR((1,)),
            ],
            compiler_params=pltpu.CompilerParams(collective_id=0, has_side_effects=True),
        )(
            normalized.reshape(examples, tokens, features),
            upstream.reshape(examples, tokens, features),
            owner_order,
            jnp.swapaxes(sketch_index, 1, 2),
            jnp.swapaxes(sketch_scale, 1, 2),
            query_sketch,
        )
        sketch, scores = pl.pallas_call(
            put_out,
            out_shape=(
                jax.ShapeDtypeStruct(sketch.shape, sketch.dtype),
                jax.ShapeDtypeStruct(scores.shape, scores.dtype),
            ),
            in_specs=[vmem, vmem],
            out_specs=(hbm, hbm),
            scratch_shapes=[dma((2,))],
            compiler_params=pltpu.CompilerParams(vmem_limit_bytes=1 << 20),
        )(sketch, scores)
        return sketch, scores.T

    placed = (
        P("ex", "lay", None, "col"),
        P("ex", "lay", None, "col"),
        P("ex", None),
        P(None, "col", None),
        P(None, "col", None),
        P("ex", "col"),
    )
    return jax.shard_map(
        local,
        mesh=mesh,
        in_specs=placed,
        out_specs=(P(("ex", "lay"), "col"), P(("ex", "lay"), "col")),
        check_vma=False,
    )
```

time: 13.3 us -> 11.4 us (0.86)
  local copies, waits for them, and re-layouts: 1.17 us -> 0 us
  Pallas kernels: 11.4 us -> 10.6 us
    pallas_call x1, Pallas kernels: 11.4 us -> 9.97 us  [local(): pl.pallas_call(functools.partial(kernel, (n_ex, n_col, n_lay, per_col, k_...]
    unnamed x2 -> x0, local copies, waits for them, and re-layouts: 1.17 us -> none
    pallas_call x0 -> x1, Pallas kernels: none -> 0.68 us  [local(): pl.pallas_call(put_out, out_shape=(jax.ShapeDtypeStruct(sketch.shape, ske...]
where the time goes in v1:
time: 11.4 us; the launch traced here: 11.3 us
  Pallas kernels  10.6 us (93%)
  between operations  0.64 us (6%)
    pallas_call x1, Pallas kernels, local(): pl.pallas_call(functools.partial(kernel, (n_ex, n_col, n_lay, per_col, k_...  9.97 us
    pallas_call x1, Pallas kernels, local(): pl.pallas_call(put_out, out_shape=(jax.ShapeDtypeStruct(sketch.shape, ske...  0.68 us

profile of v1, /device:TPU:0, one launch (start us, length us, event | category | flops | bytes accessed | tf_op | source)
XLA Modules:
  0.0 11.3 jit_solution(573705881923075643)
XLA Ops:
  0.6 10.0 %shard_map.77 = (bf16[32,2048]{1,0:T(8,128)(2,1)S(1)}, f32[1,32]{1,0:T(1,128)S(1)}) custom-call(bf16[64,4,896]{2,1,0:T(4,128)(2,1)} %bitcast.5, bf16[64,4,896]{2,1,0:T(4,128)(2,1)} %bitcast.6, s32[1,64]{1,0:T(1,128)} %order_hbm.1, s32[2,4,7]{2,1,0:T(4,128)} %bitcast.7, bf16[2,4,7]{2,1,0:T(4,128)(2,1)} %bitcast.8, bf16[1,2048]{1,0:T(2,128)(2,1)} %query_hbm.1), custom_call_target="tpu_custom_call" | custom-call | tf_op jit(solution)/shard_map/pallas_call | solution.py:493
  10.6 0.7 %shard_map.78 = (bf16[32,2048]{1,0:T(8,128)(2,1)}, f32[1,32]{1,0:T(1,128)}) custom-call(bf16[32,2048]{1,0:T(8,128)(2,1)S(1)} %get-tuple-element.6.sketch_ref, f32[1,32]{1,0:T(1,128)S(1)} %get-tuple-element.7.scores_ref), custom_call_target="tpu_custom_call" | custom-call | tf_op jit(solution)/shard_map/pallas_call | solution.py:540

commit v2 on v1

--- a/solution.py
+++ b/solution.py
@@ -11,14 +11,23 @@
 MESH = pl.DeviceIdType.MESH
 LANES = 128
 WAVES = 4
-GROUP = 4
 TILE = 16
+CUTS = 2
+PUT = 8
 
 
 def cuts(total):
     waves = min(WAVES, total)
     sizes = [total // waves + (i < total % waves) for i in range(waves)]
     return [(sum(sizes[:i]), sizes[i]) for i in range(waves)]
+
+
+def batches(waves):
+    heads = [(*waves[0], [0])]
+    tail = waves[1:]
+    if tail:
+        heads.append((tail[0][0], sum(count for _, count in tail), list(range(1, len(waves)))))
+    return heads
 
 
 def signs():
@@ -58,7 +67,8 @@
     splat_ref,
     turned_tab_ref,
     weights_ref,
-    rot_ref,
+    wide_ref,
+    mix_ref,
     total_ref,
     score_ref,
     load_sem,
@@ -86,9 +96,8 @@
     scale = 1.0 / math.sqrt(float(LANES))
     waves = cuts(in_blocks)
 
-    load_parts = [pl.ds(0, waves[0][1] * LANES)]
-    if len(waves) > 1:
-        load_parts.append(pl.ds(waves[1][0] * LANES, features - waves[1][0] * LANES))
+    parts = batches(waves)
+    load_parts = [pl.ds(first * LANES, count * LANES) for first, count, _ in parts]
     smalls = [
         pltpu.make_async_copy(source, held, small_sem.at[i])
         for i, (source, held) in enumerate(
@@ -126,10 +135,16 @@
             device_id_type=MESH,
         )
 
-    for dl in reversed(range(n_lay)):
-        for dc in reversed(range(n_col)):
-            if dl or dc:
-                greet(barrier, ex, lax.rem(col + dc, n_col), lax.rem(lay + dl, n_lay))
+    def greet_chip(sem):
+        def body(target, carry):
+            for odd in range(2):
+                greet(sem, ex, 2 * lax.rem(target, half) + odd, target // half)
+            return carry
+
+        return body
+
+    greet(barrier, ex, sibling, lay)
+    lax.fori_loop(chip + 1, others + 1, greet_chip(barrier), 0)
 
     def greet_askers(at_ex, carry):
         greet(barrier, at_ex, asker, lay)
@@ -148,7 +163,13 @@
         jnp.maximum(ex + 1, asked_first), asked_first + per_col, greet_sources(barrier), 0
     )
     below = jnp.clip(ex - asked_first, 0, per_col)
-    greetings = n_lay * n_col - 1 + ex + n_col * below
+    greetings = 1 + 2 * chip + ex + n_col * below
+
+    pl.semaphore_wait(barrier, greetings)
+    lax.fori_loop(0, chip, greet_chip(ready_sem.at[1]), 0)
+    lax.fori_loop(
+        asked_first, jnp.minimum(asked_first + per_col, ex), greet_sources(ready_sem.at[0]), 0
+    )
 
     had_ref[...] = signs()
     own_tab_ref[...] = jnp.full(own_tab_ref.shape, -1.0, jnp.float32)
@@ -216,6 +237,75 @@
         == order_ref[...]
     ).astype(jnp.float32)
     chosen = chosen.T.astype(jnp.bfloat16)
+
+    def make(k):
+        first, count, _ = parts[k]
+        part = load_parts[k]
+        pltpu.make_async_copy(
+            xu_ref.at[:, :, :, part], xu_ref.at[:, :, :, part], load_sem.at[k]
+        ).wait()
+        x, u = (
+            xu_ref[i, :, :, first * LANES : (first + count) * LANES]
+            .reshape(examples * tokens, count * LANES)
+            .astype(jnp.float32)
+            for i in range(2)
+        )
+        product = x * u
+        high = product.astype(jnp.bfloat16)
+        low = (product - high.astype(jnp.float32)).astype(jnp.bfloat16)
+        ordered = (
+            jnp.dot(chosen, high, preferred_element_type=jnp.float32)
+            + jnp.dot(chosen, low, preferred_element_type=jnp.float32)
+        ).astype(jnp.bfloat16)
+        stacked = jnp.concatenate(
+            [ordered[:, b * LANES : (b + 1) * LANES] for b in range(count)], axis=0
+        )
+        stacked = turn(stacked).astype(jnp.bfloat16)
+        for owner in range(n_lay):
+            for b in range(count):
+                at = b * examples + owner * rows
+                owned_ref[owner, first + b] = stacked[at : at + rows]
+
+    place = lax.rem(ex, per_col) * n_col + col
+    mine = asker == col
+
+    def query_copy(target):
+        return pltpu.make_async_remote_copy(
+            src_ref=own_query_ref,
+            dst_ref=queries_ref.at[place],
+            send_sem=query_sem.at[0],
+            recv_sem=query_sem.at[1],
+            device_id={"ex": target, "col": asker, "lay": lay},
+            device_id_type=MESH,
+        )
+
+    def send_query(target, carry):
+        query_copy(target).start()
+        return carry
+
+    def send_pieces(ks):
+        def body(number, carry):
+            for k in ks:
+                piece_copy(k, number).start()
+            return carry
+
+        return body
+
+    def send_first(k):
+        @pl.when(chip > 0)
+        def _():
+            for wave in parts[k][2]:
+                piece_copy(wave, 0).start()
+
+        own_copy(*parts[k][:2]).start()
+
+    def tabs_to(wanted):
+        for dc in range(1, n_col):
+            target = lax.rem(col + dc, n_col)
+            pl.when(wanted(target // 2, col // 2))(lambda: tab_copy(dc).start())
+
+    make(0)
+    send_first(0)
     for copy in smalls[1:]:
         copy.wait()
     for layer in range(layers):
@@ -228,77 +318,32 @@
             jnp.float32
         )
     own_query_ref[...] = own_query_f32_ref[...].astype(jnp.bfloat16)
-
-    for k, (first, count) in enumerate(waves):
-        if k < len(load_parts):
-            part = load_parts[k]
-            pltpu.make_async_copy(
-                xu_ref.at[:, :, :, part], xu_ref.at[:, :, :, part], load_sem.at[k]
-            ).wait()
-        x, u = (
-            xu_ref[i, :, :, first * LANES : (first + count) * LANES]
-            .reshape(examples * tokens, count * LANES)
-            .astype(jnp.float32)
-            for i in range(2)
-        )
-        product = x * u
-        high = product.astype(jnp.bfloat16)
-        low = (product - high.astype(jnp.float32)).astype(jnp.bfloat16)
-        ordered = (
-            jnp.dot(chosen, high, preferred_element_type=jnp.float32)
-            + jnp.dot(chosen, low, preferred_element_type=jnp.float32)
-        ).astype(jnp.bfloat16)
-        stacked = jnp.concatenate(
-            [ordered[:, b * LANES : (b + 1) * LANES] for b in range(count)], axis=0
-        )
-        if k:
-            stacked = turn(stacked).astype(jnp.bfloat16)
-        for owner in range(n_lay):
-            for b in range(count):
-                at = b * examples + owner * rows
-                owned_ref[owner, first + b] = stacked[at : at + rows]
-        if k == 0:
-            pl.semaphore_wait(barrier, greetings)
-            lax.fori_loop(
-                asked_first,
-                jnp.minimum(asked_first + per_col, ex),
-                greet_sources(ready_sem.at[0]),
-                0,
-            )
-        if others:
-            piece_copy(k, 0).start()
-        if k == 0:
-            for dc in range(1, n_col):
-                tab_copy(dc).start()
-        else:
-            for number in range(1, others):
-                piece_copy(k - 1, number).start()
-        own_copy(first, count).start()
-    for number in range(1, others):
-        piece_copy(len(waves) - 1, number).start()
-
-    place = lax.rem(ex, per_col) * n_col + col
-    mine = asker == col
-
-    def query_copy(target):
-        return pltpu.make_async_remote_copy(
-            src_ref=own_query_ref,
-            dst_ref=queries_ref.at[place],
-            send_sem=query_sem.at[0],
-            recv_sem=query_sem.at[1],
-            device_id={"ex": target, "col": asker, "lay": lay},
-            device_id_type=MESH,
-        )
-
-    def send_query(target, carry):
-        query_copy(target).start()
-        return carry
+    tabs_to(lambda target, here: target <= here)
+    def share_query():
+        query_copy(ex).start()
+
+    here = asker // 2 <= col // 2
 
     @pl.when(mine)
     def _():
         pltpu.make_async_copy(own_query_ref, queries_ref.at[place], query_sem.at[1]).start()
 
-    pl.when(jnp.logical_not(mine))(lambda: query_copy(ex).start())
+    pl.when(jnp.logical_and(here, jnp.logical_not(mine)))(share_query)
+
+    for k in range(1, len(parts)):
+        make(k)
+        send_first(k)
+
+
+    lax.fori_loop(1, chip, send_pieces(range(len(waves))), 0)
+
+    @pl.when(chip < others)
+    def _():
+        pl.semaphore_wait(ready_sem.at[1], 2 * (others - chip))
+        tabs_to(lambda target, here: target > here)
+        lax.fori_loop(chip, others, send_pieces(range(len(waves))), 0)
+        pl.when(jnp.logical_not(here))(share_query)
+
     lax.fori_loop(0, ex, send_query, 0)
 
     def queries_up():
@@ -321,7 +366,7 @@
         return value
 
     def spread(slot):
-        own = table(slot, col * out_blocks, out_blocks) * scale
+        own = table(slot, col * out_blocks, out_blocks)
         for at_lay in range(layers):
             for b in range(in_blocks):
                 at = stride * at_lay + b
@@ -329,39 +374,69 @@
                     own[:, at : at + 1], (out_blocks, LANES)
                 )
 
-    metas = []
-
-    def combine(source, blocks, turned, first=False, last=False):
-        base, count = len(metas), len(blocks)
+    edge = min(rows, TILE)
+    folds = rows // edge
+    across = LANES // edge
+    metas, bases = [], {}
+
+    def prepare(name, blocks):
+        base = sum(-(-len(held) // across) for held, _, _ in bases.values())
+        bases[name] = (blocks, base, len(metas))
         metas.extend(blocks)
-        if turned:
-            rot_ref[base : base + count] = source.astype(jnp.float32)
-        else:
-            rot_ref[base : base + count] = turn(source.reshape(count * rows, LANES)).reshape(
-                count, rows, LANES
-            )
-        for o in range(0, out_blocks, GROUP):
-            if first:
-                sums = [jnp.zeros((rows, LANES), jnp.float32) for _ in range(GROUP)]
-            else:
-                sums = [total_ref[o + g] for g in range(GROUP)]
-            for i, (at_lay, slot, b) in enumerate(blocks):
-                value = rot_ref[base + i]
-                for g in range(GROUP):
-                    sums[g] = sums[g] + value * splat_ref[at_lay, slot, b, o + g : o + g + 1, :]
-            for g in range(GROUP):
-                if last:
-                    sketch_ref[:, (o + g) * LANES : (o + g + 1) * LANES] = sums[g].astype(
-                        jnp.bfloat16
-                    )
-                else:
-                    total_ref[o + g] = sums[g]
+        lane = lax.broadcasted_iota(jnp.int32, (out_blocks, LANES), 1) // edge
+        same = lax.rem(lax.broadcasted_iota(jnp.int32, (edge, LANES), 1), edge) == (
+            lax.broadcasted_iota(jnp.int32, (edge, LANES), 0)
+        )
+        for t in range(0, len(blocks), across):
+            wide = jnp.zeros((out_blocks, LANES), jnp.float32)
+            for i, (at_lay, slot, b) in enumerate(blocks[t : t + across]):
+                wide = jnp.where(lane == i, splat_ref[at_lay, slot, b], wide)
+            tile = base + t // across
+            wide_ref[tile] = wide
+            for o in range(out_blocks):
+                mix_ref[tile, o * edge : (o + 1) * edge, :] = jnp.where(
+                    same, jnp.broadcast_to(wide_ref[tile, o : o + 1, :], (edge, LANES)), 0.0
+                ).astype(jnp.bfloat16)
+
+    def combine(name, source, first=False, last=False):
+        blocks, base, _ = bases[name]
+        folded = jnp.concatenate(
+            [
+                source[:, h * edge : (h + 1) * edge, :].reshape(len(blocks) * edge, LANES)
+                for h in range(folds)
+            ],
+            axis=1,
+        )
+        cut = out_blocks // CUTS
+        for low in range(0, out_blocks, cut):
+            part = slice(low * edge, (low + cut) * edge)
+            value = None
+            for t in range(0, len(blocks), across):
+                width = min(across, len(blocks) - t) * edge
+                term = jnp.dot(
+                    mix_ref[base + t // across, part, :width],
+                    folded[t * edge : t * edge + width],
+                    preferred_element_type=jnp.float32,
+                )
+                value = term if value is None else value + term
+            if not first:
+                value = value + total_ref[part]
+            if not last:
+                total_ref[part] = value
+                continue
+            value = value * scale
+            for o in range(cut):
+                at = slice((low + o) * LANES, (low + o + 1) * LANES)
+                for h in range(folds):
+                    sketch_ref[h * edge : (h + 1) * edge, at] = value[
+                        o * edge : (o + 1) * edge, h * LANES : (h + 1) * LANES
+                    ].astype(jnp.bfloat16)
 
     def await_wave(k):
         part = arrived_ref.at[wave_part(k)]
         to_sibling(part, part, send_sem.at[2], wave_sem.at[k]).wait_recv()
 
-    def combine_wave(k, last=False):
+    def wave_blocks(k):
         first, count = waves[k]
         blocks = []
         for number in range(others):
@@ -369,37 +444,54 @@
             for odd in range(2):
                 slot = slot_of(2 * lax.rem(source, half) + odd)
                 blocks += [(source // half, slot, first + b) for b in range(count)]
+        return blocks
+
+    def add_scores(name, source):
+        blocks = bases[name][0]
+        for q in range(per_col):
+            value = score_ref[q]
+            for i, (at_lay, slot, b) in enumerate(blocks):
+                value = value + source[i].astype(jnp.float32) * weights_ref[
+                    slot, at_lay, b : b + 1, q * LANES : (q + 1) * LANES
+                ]
+            score_ref[q] = value
+
+    def wave_values(k):
+        first, count = waves[k]
         low = 2 * others * first
-        combine(arrived_ref[low : low + 2 * others * count], blocks, k > 0, last=last)
-        add_scores(len(metas) - len(blocks), len(metas))
-
-    early = waves[0][1]
+        return arrived_ref[low : low + 2 * others * count]
+
     spread(0)
-    combine(owned_ref[lay, :early], [(lay, 0, b) for b in range(early)], False, first=True)
-    combine(owned_ref[lay, early:], [(lay, 0, b) for b in range(early, in_blocks)], True)
+    prepare("own", [(lay, 0, b) for b in range(in_blocks)])
+    combine("own", owned_ref[lay], first=True)
+    near = slot_of(sibling)
+
+    odd_core = core == 1
+
+    def take(k):
+        await_wave(k)
+        relay_copy(k).start()
+
+    pl.when(chip > 0)(queries_up)
+    pl.when(odd_core)(lambda: take(0))
 
     all_tabs().wait_recv()
     for slot in range(1, n_col):
         spread(slot)
+    prepare("sibling", [(lay, near, b) for b in range(in_blocks)])
+    for k in range(len(waves)):
+        prepare(k, wave_blocks(k))
     to_sibling(sibling_ref, sibling_ref, send_sem.at[1], sibling_sem.at[0]).wait_recv()
-    near = slot_of(sibling)
-    combine(sibling_ref[:early], [(lay, near, b) for b in range(early)], False)
-    combine(sibling_ref[early:], [(lay, near, b) for b in range(early, in_blocks)], True)
+    combine("sibling", sibling_ref[...])
     for slot in range(n_col):
         whole = table(slot, 0, n_col * out_blocks).T
         turned_tab_ref[slot] = whole.astype(jnp.bfloat16)
 
-    def add_scores(start, stop):
+    def put_scores():
         for q in range(per_col):
-            value = score_ref[q]
-            for i in range(start, stop):
-                at_lay, slot, b = metas[i]
-                value = value + rot_ref[i] * weights_ref[
-                    slot, at_lay, b : b + 1, q * LANES : (q + 1) * LANES
-                ]
-            score_ref[q] = value
-
-    def start_scores(stop):
+            scores_ref[q : q + 1, :] = jnp.sum(score_ref[q].T, axis=0, keepdims=True) * scale
+
+    def start_scores():
         pltpu.make_async_copy(queries_ref, queries_ref, query_sem.at[1]).wait()
         asked = jnp.concatenate(
             [
@@ -416,32 +508,42 @@
             preferred_element_type=jnp.float32,
         ).reshape(weights_ref.shape)
         score_ref[...] = jnp.zeros_like(score_ref)
-        add_scores(0, stop)
-
-    timely = jnp.logical_and(asked_first == ex, per_col == 1)
-
-    @pl.when(timely)
-    def _():
-        start_scores(2 * in_blocks)
+        add_scores("own", owned_ref[lay])
+        add_scores("sibling", sibling_ref[...])
+
+    timely = asked_first >= ex
 
     @pl.when(jnp.logical_not(timely))
     def _():
         weights_ref[...] = jnp.zeros_like(weights_ref)
         score_ref[...] = jnp.zeros_like(score_ref)
 
-    odd_core = core == 1
-    pl.when(jnp.logical_not(odd_core))(queries_up)
+    pl.when(jnp.logical_and(timely, jnp.logical_not(odd_core)))(start_scores)
+    pl.when(chip == 0)(queries_up)
     last = len(waves) - 1
     for k in range(len(waves)):
-        await_wave(k)
-        pl.when(odd_core)(lambda: relay_copy(k).start())
-        combine_wave(k, last=k == last)
         if k == 0:
-            pl.when(odd_core)(queries_up)
-
-    pl.when(jnp.logical_not(timely))(lambda: start_scores(len(metas)))
-    for q in range(per_col):
-        scores_ref[q : q + 1, :] = jnp.sum(score_ref[q].T, axis=0, keepdims=True) * scale
+
+            @pl.when(odd_core)
+            def _():
+                for later in range(1, len(waves)):
+                    take(later)
+                pl.when(timely)(start_scores)
+
+        pl.when(jnp.logical_not(odd_core))(lambda: await_wave(k))
+        if k == last:
+            add_scores(k, wave_values(k))
+            put_scores()
+        combine(k, wave_values(k), last=k == last)
+        if k < last:
+            add_scores(k, wave_values(k))
+
+    @pl.when(jnp.logical_not(timely))
+    def _():
+        start_scores()
+        for k in range(len(waves)):
+            add_scores(k, wave_values(k))
+        put_scores()
 
     part = arrived_ref.at[pl.ds(0, others * in_blocks)]
     to_sibling(part, part, send_sem.at[0], wave_sem.at[0]).wait_send()
@@ -462,14 +564,13 @@
 
 
 def put_out(sketch_ref, scores_ref, sketch_hbm, scores_hbm, sem):
-    copies = [
-        pltpu.make_async_copy(sketch_ref, sketch_hbm, sem.at[0]),
-        pltpu.make_async_copy(scores_ref, scores_hbm, sem.at[1]),
-    ]
-    for copy in copies:
-        copy.start()
-    for copy in copies:
-        copy.wait()
+    for first in range(0, sketch_ref.shape[0], PUT):
+        part = pl.ds(first, PUT)
+        pltpu.make_async_copy(sketch_ref.at[part], sketch_hbm.at[part], sem.at[0]).start()
+    scores = pltpu.make_async_copy(scores_ref, scores_hbm, sem.at[1])
+    scores.start()
+    pltpu.make_async_copy(sketch_ref, sketch_hbm, sem.at[0]).wait()
+    scores.wait()
 
 
 def solution(mesh):
@@ -487,6 +588,9 @@
         rows = examples // n_lay
         waves = len(cuts(in_blocks))
         others = n_lay * n_col // 2 - 1
+        edge = min(rows, TILE)
+        groups = [in_blocks] * 2 + [2 * others * count for _, count in cuts(in_blocks)]
+        tiles = sum(-(-blocks * edge // LANES) for blocks in groups)
         vmem = pl.BlockSpec(memory_space=pltpu.VMEM)
         hbm = pl.BlockSpec(memory_space=pl.ANY)
         dma = pltpu.SemaphoreType.DMA
@@ -516,8 +620,9 @@
                 pltpu.VMEM((layers, n_col, in_blocks, out_blocks, LANES), jnp.float32),
                 pltpu.VMEM((n_col, LANES, n_col * out_blocks), jnp.bfloat16),
                 pltpu.VMEM((n_col, layers, LANES // layers, per_col * LANES), jnp.float32),
-                pltpu.VMEM((n_lay * n_col * in_blocks, rows, LANES), jnp.float32),
-                pltpu.VMEM((out_blocks, rows, LANES), jnp.float32),
+                pltpu.VMEM((tiles, out_blocks, LANES), jnp.float32),
+                pltpu.VMEM((tiles, out_blocks * edge, LANES), jnp.bfloat16),
+                pltpu.VMEM((out_blocks * edge, rows // edge * LANES), jnp.float32),
                 pltpu.VMEM((per_col, rows, LANES), jnp.float32),
                 dma((min(waves, 2),)),
                 dma((4,)),
@@ -526,7 +631,7 @@
                 dma((1,)),
                 dma((2,)),
                 dma((2,)),
-                pltpu.SemaphoreType.REGULAR((1,)),
+                pltpu.SemaphoreType.REGULAR((2,)),
             ],
             compiler_params=pltpu.CompilerParams(collective_id=0, has_side_effects=True),
         )(

time: 11.4 us -> 10.7 us (0.939)
  the two profiles are of different devices: /device:TPU:0 before, /device:TPU:5 now
where the time goes in v2:
time: 10.7 us; the launch traced here: 10.5 us
  Pallas kernels  9.88 us (92%)
  between operations  0.64 us (6%)
    pallas_call x1, Pallas kernels, local(): pl.pallas_call(functools.partial(kernel, (n_ex, n_col, n_lay, per_col, k_...  9.21 us
    pallas_call x1, Pallas kernels, local(): pl.pallas_call(put_out, out_shape=(jax.ShapeDtypeStruct(sketch.shape, ske...  0.67 us

profile of v2, /device:TPU:5, one launch (start us, length us, event | category | flops | bytes accessed | tf_op | source)
XLA Modules:
  0.0 10.5 jit_solution(12941422251443182785)
XLA Ops:
  0.6 9.2 %shard_map.77 = (bf16[32,2048]{1,0:T(8,128)(2,1)S(1)}, f32[1,32]{1,0:T(1,128)S(1)}) custom-call(bf16[64,4,896]{2,1,0:T(4,128)(2,1)} %bitcast.5, bf16[64,4,896]{2,1,0:T(4,128)(2,1)} %bitcast.6, s32[1,64]{1,0:T(1,128)} %order_hbm.1, s32[2,4,7]{2,1,0:T(4,128)} %bitcast.7, bf16[2,4,7]{2,1,0:T(4,128)(2,1)} %bitcast.8, bf16[1,2048]{1,0:T(2,128)(2,1)} %query_hbm.1), custom_call_target="tpu_custom_call" | custom-call | tf_op jit(solution)/shard_map/pallas_call | solution.py:597
  9.8 0.7 %shard_map.78 = (bf16[32,2048]{1,0:T(8,128)(2,1)}, f32[1,32]{1,0:T(1,128)}) custom-call(bf16[32,2048]{1,0:T(8,128)(2,1)S(1)} %get-tuple-element.6.sketch_ref, f32[1,32]{1,0:T(1,128)S(1)} %get-tuple-element.7.scores_ref), custom_call_target="tpu_custom_call" | custom-call | tf_op jit(solution)/shard_map/pallas_call | solution.py:645

commit v3 on v2

--- a/solution.py
+++ b/solution.py
@@ -88,6 +88,7 @@
     in_blocks = features // LANES
     layers = index_ref.shape[0]
     stride = LANES // layers
+    padded = weights_ref.shape[2]
     out_blocks = query_ref.shape[1] // LANES
     half = n_col // 2
     others = n_lay * half - 1
@@ -95,6 +96,50 @@
     sibling = col + 1 - 2 * core
     scale = 1.0 / math.sqrt(float(LANES))
     waves = cuts(in_blocks)
+
+    barrier = pltpu.get_barrier_semaphore()
+    asker = ex // per_col
+    asked_first = col * per_col
+
+    def greet(sem, at_ex, at_col, at_lay):
+        pl.semaphore_signal(
+            sem,
+            inc=1,
+            device_id={"ex": at_ex, "col": at_col, "lay": at_lay},
+            device_id_type=MESH,
+        )
+
+    def greet_chip(sem, target):
+        for odd in range(2):
+            greet(sem, ex, 2 * lax.rem(target, half) + odd, target // half)
+
+    def greet_chips(sem, start, stop):
+        def body(target, carry):
+            greet_chip(sem, target)
+            return carry
+
+        lax.fori_loop(start, stop, body, 0)
+
+    def greet_askers(at_ex, carry):
+        greet(barrier, at_ex, asker, lay)
+        return carry
+
+    def greet_sources(sem):
+        def body(at_ex, carry):
+            for at_col in range(n_col):
+                greet(sem, at_ex, at_col, lay)
+            return carry
+
+        return body
+
+    below = jnp.clip(ex - asked_first, 0, per_col)
+    greeted = jnp.where(chip == others, others, jnp.minimum(chip, 1))
+    greetings = 1 + 2 * greeted + ex + n_col * below
+
+    def known(target):
+        return jnp.logical_or(
+            target == chip, jnp.logical_or(chip == others, jnp.logical_and(target == 0, chip > 0))
+        )
 
     parts = batches(waves)
     load_parts = [pl.ds(first * LANES, count * LANES) for first, count, _ in parts]
@@ -123,50 +168,16 @@
             for copy in smalls[1:]:
                 copy.start()
 
-    barrier = pltpu.get_barrier_semaphore()
-    asker = ex // per_col
-    asked_first = col * per_col
-
-    def greet(sem, at_ex, at_col, at_lay):
-        pl.semaphore_signal(
-            sem,
-            inc=1,
-            device_id={"ex": at_ex, "col": at_col, "lay": at_lay},
-            device_id_type=MESH,
-        )
-
-    def greet_chip(sem):
-        def body(target, carry):
-            for odd in range(2):
-                greet(sem, ex, 2 * lax.rem(target, half) + odd, target // half)
-            return carry
-
-        return body
-
+    pl.when(chip == 0)(lambda: greet_chips(barrier, 1, others + 1))
+    pl.when(jnp.logical_and(chip > 0, chip < others))(lambda: greet_chip(barrier, others))
     greet(barrier, ex, sibling, lay)
-    lax.fori_loop(chip + 1, others + 1, greet_chip(barrier), 0)
-
-    def greet_askers(at_ex, carry):
-        greet(barrier, at_ex, asker, lay)
-        return carry
-
-    def greet_sources(sem):
-        def body(at_ex, carry):
-            for at_col in range(n_col):
-                greet(sem, at_ex, at_col, lay)
-            return carry
-
-        return body
-
     lax.fori_loop(ex + 1, n_ex, greet_askers, 0)
     lax.fori_loop(
         jnp.maximum(ex + 1, asked_first), asked_first + per_col, greet_sources(barrier), 0
     )
-    below = jnp.clip(ex - asked_first, 0, per_col)
-    greetings = 1 + 2 * chip + ex + n_col * below
-
     pl.semaphore_wait(barrier, greetings)
-    lax.fori_loop(0, chip, greet_chip(ready_sem.at[1]), 0)
+    pl.when(jnp.logical_and(chip > 0, chip < others))(lambda: greet_chip(ready_sem.at[1], 0))
+    pl.when(chip == others)(lambda: greet_chips(ready_sem.at[1], 0, others))
     lax.fori_loop(
         asked_first, jnp.minimum(asked_first + per_col, ex), greet_sources(ready_sem.at[0]), 0
     )
@@ -210,12 +221,12 @@
     def own_copy(first, count):
         part = pl.ds(first, count)
         return to_sibling(
-            owned_ref.at[lay, part], sibling_ref.at[part], send_sem.at[1], sibling_sem.at[0]
+            owned_ref.at[lay, part], sibling_ref.at[part], send_sem.at[0], sibling_sem.at[0]
         )
 
     def relay_copy(k):
         part = arrived_ref.at[wave_part(k)]
-        return to_sibling(part, part, send_sem.at[2], wave_sem.at[k])
+        return to_sibling(part, part, send_sem.at[1], wave_sem.at[k])
 
     def tab_copy(dc):
         return pltpu.make_async_remote_copy(
@@ -244,27 +255,27 @@
         pltpu.make_async_copy(
             xu_ref.at[:, :, :, part], xu_ref.at[:, :, :, part], load_sem.at[k]
         ).wait()
-        x, u = (
-            xu_ref[i, :, :, first * LANES : (first + count) * LANES]
-            .reshape(examples * tokens, count * LANES)
-            .astype(jnp.float32)
-            for i in range(2)
-        )
-        product = x * u
-        high = product.astype(jnp.bfloat16)
-        low = (product - high.astype(jnp.float32)).astype(jnp.bfloat16)
-        ordered = (
-            jnp.dot(chosen, high, preferred_element_type=jnp.float32)
-            + jnp.dot(chosen, low, preferred_element_type=jnp.float32)
-        ).astype(jnp.bfloat16)
-        stacked = jnp.concatenate(
-            [ordered[:, b * LANES : (b + 1) * LANES] for b in range(count)], axis=0
-        )
-        stacked = turn(stacked).astype(jnp.bfloat16)
-        for owner in range(n_lay):
-            for b in range(count):
-                at = b * examples + owner * rows
-                owned_ref[owner, first + b] = stacked[at : at + rows]
+        ordered = []
+        for b in range(first, first + count):
+            x, u = (
+                xu_ref[i, :, :, b * LANES : (b + 1) * LANES]
+                .reshape(examples * tokens, LANES)
+                .astype(jnp.float32)
+                for i in range(2)
+            )
+            product = x * u
+            high = product.astype(jnp.bfloat16)
+            low = (product - high.astype(jnp.float32)).astype(jnp.bfloat16)
+            ordered.append(
+                (
+                    jnp.dot(chosen, high, preferred_element_type=jnp.float32)
+                    + jnp.dot(chosen, low, preferred_element_type=jnp.float32)
+                ).astype(jnp.bfloat16)
+            )
+        for b in range(count):
+            stacked = turn(ordered[b]).astype(jnp.bfloat16)
+            for owner in range(n_lay):
+                owned_ref[owner, first + b] = stacked[owner * rows : (owner + 1) * rows]
 
     place = lax.rem(ex, per_col) * n_col + col
     mine = asker == col
@@ -299,10 +310,10 @@
 
         own_copy(*parts[k][:2]).start()
 
-    def tabs_to(wanted):
+    def tabs_to(greeted):
         for dc in range(1, n_col):
-            target = lax.rem(col + dc, n_col)
-            pl.when(wanted(target // 2, col // 2))(lambda: tab_copy(dc).start())
+            target = lay * half + lax.rem(col + dc, n_col) // 2
+            pl.when(known(target) == greeted)(lambda: tab_copy(dc).start())
 
     make(0)
     send_first(0)
@@ -318,11 +329,11 @@
             jnp.float32
         )
     own_query_ref[...] = own_query_f32_ref[...].astype(jnp.bfloat16)
-    tabs_to(lambda target, here: target <= here)
+    tabs_to(True)
     def share_query():
         query_copy(ex).start()
 
-    here = asker // 2 <= col // 2
+    here = known(lay * half + asker // 2)
 
     @pl.when(mine)
     def _():
@@ -335,14 +346,13 @@
         send_first(k)
 
 
-    lax.fori_loop(1, chip, send_pieces(range(len(waves))), 0)
-
     @pl.when(chip < others)
     def _():
-        pl.semaphore_wait(ready_sem.at[1], 2 * (others - chip))
-        tabs_to(lambda target, here: target > here)
-        lax.fori_loop(chip, others, send_pieces(range(len(waves))), 0)
+        pl.semaphore_wait(ready_sem.at[1], jnp.where(chip == 0, 2 * others, 2))
+        tabs_to(False)
         pl.when(jnp.logical_not(here))(share_query)
+
+        lax.fori_loop(jnp.minimum(chip, 1), others, send_pieces(range(len(waves))), 0)
 
     lax.fori_loop(0, ex, send_query, 0)
 
@@ -398,7 +408,10 @@
                     same, jnp.broadcast_to(wide_ref[tile, o : o + 1, :], (edge, LANES)), 0.0
                 ).astype(jnp.bfloat16)
 
-    def combine(name, source, first=False, last=False):
+    cut = out_blocks // CUTS
+    cut_rows = [slice(low * edge, (low + cut) * edge) for low in range(0, out_blocks, cut)]
+
+    def combine(name, source, sums):
         blocks, base, _ = bases[name]
         folded = jnp.concatenate(
             [
@@ -407,10 +420,8 @@
             ],
             axis=1,
         )
-        cut = out_blocks // CUTS
-        for low in range(0, out_blocks, cut):
-            part = slice(low * edge, (low + cut) * edge)
-            value = None
+        result = []
+        for part, value in zip(cut_rows, sums):
             for t in range(0, len(blocks), across):
                 width = min(across, len(blocks) - t) * edge
                 term = jnp.dot(
@@ -419,22 +430,26 @@
                     preferred_element_type=jnp.float32,
                 )
                 value = term if value is None else value + term
-            if not first:
-                value = value + total_ref[part]
-            if not last:
-                total_ref[part] = value
-                continue
-            value = value * scale
-            for o in range(cut):
-                at = slice((low + o) * LANES, (low + o + 1) * LANES)
-                for h in range(folds):
-                    sketch_ref[h * edge : (h + 1) * edge, at] = value[
-                        o * edge : (o + 1) * edge, h * LANES : (h + 1) * LANES
-                    ].astype(jnp.bfloat16)
+            result.append(value)
+        return result
+
+    def put_sketch(sums):
+        for i, value in enumerate(sums):
+            value = (value + total_ref[cut_rows[i]]) * scale
+            at = slice(cut * i * LANES, cut * (i + 1) * LANES)
+            for h in range(folds):
+                for r in range(0, edge, PUT):
+                    sketch_ref[h * edge + r : h * edge + r + PUT, at] = jnp.concatenate(
+                        [
+                            value[o * edge + r : o * edge + r + PUT, h * LANES : (h + 1) * LANES]
+                            for o in range(cut)
+                        ],
+                        axis=1,
+                    ).astype(jnp.bfloat16)
 
     def await_wave(k):
         part = arrived_ref.at[wave_part(k)]
-        to_sibling(part, part, send_sem.at[2], wave_sem.at[k]).wait_recv()
+        to_sibling(part, part, send_sem.at[1], wave_sem.at[k]).wait_recv()
 
     def wave_blocks(k):
         first, count = waves[k]
@@ -447,7 +462,7 @@
         return blocks
 
     def add_scores(name, source):
-        blocks = bases[name][0]
+        blocks, values = bases[name][0], []
         for q in range(per_col):
             value = score_ref[q]
             for i, (at_lay, slot, b) in enumerate(blocks):
@@ -455,6 +470,8 @@
                     slot, at_lay, b : b + 1, q * LANES : (q + 1) * LANES
                 ]
             score_ref[q] = value
+            values.append(value)
+        return values
 
     def wave_values(k):
         first, count = waves[k]
@@ -463,7 +480,13 @@
 
     spread(0)
     prepare("own", [(lay, 0, b) for b in range(in_blocks)])
-    combine("own", owned_ref[lay], first=True)
+    none = [None] * CUTS
+    for part, value in zip(cut_rows, combine("own", owned_ref[lay], none)):
+        total_ref[part] = value
+    @pl.when(chip == others)
+    def _():
+        lax.fori_loop(1, others, send_pieces(range(len(waves))), 0)
+
     near = slot_of(sibling)
 
     odd_core = core == 1
@@ -481,29 +504,30 @@
     prepare("sibling", [(lay, near, b) for b in range(in_blocks)])
     for k in range(len(waves)):
         prepare(k, wave_blocks(k))
-    to_sibling(sibling_ref, sibling_ref, send_sem.at[1], sibling_sem.at[0]).wait_recv()
-    combine("sibling", sibling_ref[...])
+    to_sibling(sibling_ref, sibling_ref, send_sem.at[0], sibling_sem.at[0]).wait_recv()
+    for part, value in zip(cut_rows, combine("sibling", sibling_ref[...], none)):
+        total_ref[part] = total_ref[part] + value
     for slot in range(n_col):
         whole = table(slot, 0, n_col * out_blocks).T
-        turned_tab_ref[slot] = whole.astype(jnp.bfloat16)
-
-    def put_scores():
-        for q in range(per_col):
-            scores_ref[q : q + 1, :] = jnp.sum(score_ref[q].T, axis=0, keepdims=True) * scale
+        for at_lay in range(layers):
+            at = stride * at_lay
+            turned_tab_ref[slot, at_lay] = whole[at : at + padded].astype(jnp.bfloat16)
+
+    def put_scores(values):
+        for q, value in enumerate(values):
+            scores_ref[q : q + 1, :] = jnp.sum(value.T, axis=0, keepdims=True) * scale
 
     def start_scores():
         pltpu.make_async_copy(queries_ref, queries_ref, query_sem.at[1]).wait()
         asked = jnp.concatenate(
             [
-                queries_ref[j * n_col : (j + 1) * n_col]
-                .astype(jnp.float32)
-                .reshape(n_col * out_blocks, LANES)
+                queries_ref[j * n_col : (j + 1) * n_col].reshape(n_col * out_blocks, LANES)
                 for j in range(per_col)
             ],
             axis=1,
-        ).astype(jnp.bfloat16)
+        )
         weights_ref[...] = jnp.dot(
-            turned_tab_ref[...].reshape(n_col * LANES, n_col * out_blocks),
+            turned_tab_ref[...].reshape(n_col * layers * padded, n_col * out_blocks),
             asked,
             preferred_element_type=jnp.float32,
         ).reshape(weights_ref.shape)
@@ -511,7 +535,9 @@
         add_scores("own", owned_ref[lay])
         add_scores("sibling", sibling_ref[...])
 
-    timely = asked_first >= ex
+    timely = jnp.logical_or(
+        asked_first == ex, jnp.logical_and(asked_first > ex, jnp.logical_not(odd_core))
+    )
 
     @pl.when(jnp.logical_not(timely))
     def _():
@@ -521,6 +547,7 @@
     pl.when(jnp.logical_and(timely, jnp.logical_not(odd_core)))(start_scores)
     pl.when(chip == 0)(queries_up)
     last = len(waves) - 1
+    sums = none
     for k in range(len(waves)):
         if k == 0:
 
@@ -532,9 +559,10 @@
 
         pl.when(jnp.logical_not(odd_core))(lambda: await_wave(k))
         if k == last:
-            add_scores(k, wave_values(k))
-            put_scores()
-        combine(k, wave_values(k), last=k == last)
+            put_scores(add_scores(k, wave_values(k)))
+        sums = combine(k, wave_values(k), sums)
+        if k == last:
+            put_sketch(sums)
         if k < last:
             add_scores(k, wave_values(k))
 
@@ -542,17 +570,16 @@
     def _():
         start_scores()
         for k in range(len(waves)):
-            add_scores(k, wave_values(k))
-        put_scores()
-
-    part = arrived_ref.at[pl.ds(0, others * in_blocks)]
+            values = add_scores(k, wave_values(k))
+        put_scores(values)
+
+    part = arrived_ref.at[pl.ds(0, (others + 1) * in_blocks)]
     to_sibling(part, part, send_sem.at[0], wave_sem.at[0]).wait_send()
-    to_sibling(sibling_ref, sibling_ref, send_sem.at[1], sibling_sem.at[0]).wait_send()
     all_tabs().wait_send()
 
     @pl.when(odd_core)
     def _():
-        to_sibling(arrived_ref, arrived_ref, send_sem.at[2], wave_sem.at[0]).wait_send()
+        to_sibling(arrived_ref, arrived_ref, send_sem.at[1], wave_sem.at[0]).wait_send()
 
     def sent_queries(count):
         part = queries_ref.at[pl.ds(0, count)]
@@ -589,6 +616,7 @@
         waves = len(cuts(in_blocks))
         others = n_lay * n_col // 2 - 1
         edge = min(rows, TILE)
+        padded = LANES // layers if in_blocks > TILE else TILE
         groups = [in_blocks] * 2 + [2 * others * count for _, count in cuts(in_blocks)]
         tiles = sum(-(-blocks * edge // LANES) for blocks in groups)
         vmem = pl.BlockSpec(memory_space=pltpu.VMEM)
@@ -618,15 +646,15 @@
                 pltpu.VMEM((n_ex, out_blocks, LANES), jnp.bfloat16),
                 pltpu.VMEM((LANES, LANES), jnp.bfloat16),
                 pltpu.VMEM((layers, n_col, in_blocks, out_blocks, LANES), jnp.float32),
-                pltpu.VMEM((n_col, LANES, n_col * out_blocks), jnp.bfloat16),
-                pltpu.VMEM((n_col, layers, LANES // layers, per_col * LANES), jnp.float32),
+                pltpu.VMEM((n_col, layers, padded, n_col * out_blocks), jnp.bfloat16),
+                pltpu.VMEM((n_col, layers, padded, per_col * LANES), jnp.float32),
                 pltpu.VMEM((tiles, out_blocks, LANES), jnp.float32),
                 pltpu.VMEM((tiles, out_blocks * edge, LANES), jnp.bfloat16),
                 pltpu.VMEM((out_blocks * edge, rows // edge * LANES), jnp.float32),
                 pltpu.VMEM((per_col, rows, LANES), jnp.float32),
                 dma((min(waves, 2),)),
                 dma((4,)),
-                dma((3,)),
+                dma((2,)),
                 dma((waves,)),
                 dma((1,)),
                 dma((2,)),

time: 10.7 us -> 10.5 us (0.981)
  the two profiles are of different devices: /device:TPU:5 before, /device:TPU:0 now
where the time goes in v3:
time: 10.5 us; the launch traced here: 10.3 us
  Pallas kernels  9.68 us (92%)
  between operations  0.64 us (6%)
    pallas_call x1, Pallas kernels, local(): pl.pallas_call(functools.partial(kernel, (n_ex, n_col, n_lay, per_col, k_...  9.01 us
    pallas_call x1, Pallas kernels, local(): pl.pallas_call(put_out, out_shape=(jax.ShapeDtypeStruct(sketch.shape, ske...  0.67 us

profile of v3, /device:TPU:0, one launch (start us, length us, event | category | flops | bytes accessed | tf_op | source)
XLA Modules:
  0.0 10.3 jit_solution(3578070634933317470)
XLA Ops:
  0.6 9.0 %shard_map.77 = (bf16[32,2048]{1,0:T(8,128)(2,1)S(1)}, f32[1,32]{1,0:T(1,128)S(1)}) custom-call(bf16[64,4,896]{2,1,0:T(4,128)(2,1)} %bitcast.5, bf16[64,4,896]{2,1,0:T(4,128)(2,1)} %bitcast.6, s32[1,64]{1,0:T(1,128)} %order_hbm.1, s32[2,4,7]{2,1,0:T(4,128)} %bitcast.7, bf16[2,4,7]{2,1,0:T(4,128)(2,1)} %bitcast.8, bf16[1,2048]{1,0:T(2,128)(2,1)} %query_hbm.1), custom_call_target="tpu_custom_call" | custom-call | tf_op jit(solution)/shard_map/pallas_call | solution.py:625
  9.6 0.7 %shard_map.78 = (bf16[32,2048]{1,0:T(8,128)(2,1)}, f32[1,32]{1,0:T(1,128)}) custom-call(bf16[32,2048]{1,0:T(8,128)(2,1)S(1)} %get-tuple-element.6.sketch_ref, f32[1,32]{1,0:T(1,128)S(1)} %get-tuple-element.7.scores_ref), custom_call_target="tpu_custom_call" | custom-call | tf_op jit(solution)/shard_map/pallas_call | solution.py:673

commit v4 on v3

--- a/solution.py
+++ b/solution.py
@@ -154,19 +154,20 @@
             ]
         )
     ]
-    smalls[0].start()
+    for copy in smalls:
+        copy.start()
     for k, part in enumerate(load_parts):
         for i, source in enumerate((x_hbm, u_hbm)):
-            split = source.reshape(examples // pack, pack, tokens, features)
-            for r in range(pack):
-                pltpu.make_async_copy(
-                    split.at[:, r, :, part],
-                    xu_ref.at[i, :, pl.ds(r * tokens, tokens), part],
-                    load_sem.at[k],
-                ).start()
-        if k == 0:
-            for copy in smalls[1:]:
-                copy.start()
+            tiles = examples // pack
+            split = source.reshape(tiles, pack, tokens, features)
+            step = tiles // 4 if k and tiles % 4 == 0 else tiles
+            for low in range(0, tiles, step):
+                for r in range(pack):
+                    pltpu.make_async_copy(
+                        split.at[pl.ds(low, step), r, :, part],
+                        xu_ref.at[i, pl.ds(low, step), pl.ds(r * tokens, tokens), part],
+                        load_sem.at[k],
+                    ).start()
 
     pl.when(chip == 0)(lambda: greet_chips(barrier, 1, others + 1))
     pl.when(jnp.logical_and(chip > 0, chip < others))(lambda: greet_chip(barrier, others))
@@ -315,8 +316,6 @@
             target = lay * half + lax.rem(col + dc, n_col) // 2
             pl.when(known(target) == greeted)(lambda: tab_copy(dc).start())
 
-    make(0)
-    send_first(0)
     for copy in smalls[1:]:
         copy.wait()
     for layer in range(layers):
@@ -341,6 +340,8 @@
 
     pl.when(jnp.logical_and(here, jnp.logical_not(mine)))(share_query)
 
+    make(0)
+    send_first(0)
     for k in range(1, len(parts)):
         make(k)
         send_first(k)
@@ -496,7 +497,6 @@
         relay_copy(k).start()
 
     pl.when(chip > 0)(queries_up)
-    pl.when(odd_core)(lambda: take(0))
 
     all_tabs().wait_recv()
     for slot in range(1, n_col):
@@ -553,7 +553,7 @@
 
             @pl.when(odd_core)
             def _():
-                for later in range(1, len(waves)):
+                for later in range(len(waves)):
                     take(later)
                 pl.when(timely)(start_scores)
 

time: 10.5 us -> 10.4 us (level)
  no operation moved by 1% of the time
where the time goes in v4:
time: 10.4 us; the launch traced here: 10.2 us
  Pallas kernels  9.6 us (92%)
  between operations  0.64 us (6%)
    pallas_call x1, Pallas kernels, local(): pl.pallas_call(functools.partial(kernel, (n_ex, n_col, n_lay, per_col, k_...  8.93 us
    pallas_call x1, Pallas kernels, local(): pl.pallas_call(put_out, out_shape=(jax.ShapeDtypeStruct(sketch.shape, ske...  0.67 us

profile of v4, /device:TPU:0, one launch (start us, length us, event | category | flops | bytes accessed | tf_op | source)
XLA Modules:
  0.0 10.2 jit_solution(8640681413248344786)
XLA Ops:
  0.6 8.9 %shard_map.77 = (bf16[32,2048]{1,0:T(8,128)(2,1)S(1)}, f32[1,32]{1,0:T(1,128)S(1)}) custom-call(bf16[64,4,896]{2,1,0:T(4,128)(2,1)} %bitcast.5, bf16[64,4,896]{2,1,0:T(4,128)(2,1)} %bitcast.6, s32[1,64]{1,0:T(1,128)} %order_hbm.1, s32[2,4,7]{2,1,0:T(4,128)} %bitcast.7, bf16[2,4,7]{2,1,0:T(4,128)(2,1)} %bitcast.8, bf16[1,2048]{1,0:T(2,128)(2,1)} %query_hbm.1), custom_call_target="tpu_custom_call" | custom-call | tf_op jit(solution)/shard_map/pallas_call | solution.py:625
  9.6 0.7 %shard_map.78 = (bf16[32,2048]{1,0:T(8,128)(2,1)}, f32[1,32]{1,0:T(1,128)}) custom-call(bf16[32,2048]{1,0:T(8,128)(2,1)S(1)} %get-tuple-element.6.sketch_ref, f32[1,32]{1,0:T(1,128)S(1)} %get-tuple-element.7.scores_ref), custom_call_target="tpu_custom_call" | custom-call | tf_op jit(solution)/shard_map/pallas_call | solution.py:673

commit v5 on v4

--- a/solution.py
+++ b/solution.py
@@ -12,7 +12,7 @@
 LANES = 128
 WAVES = 4
 TILE = 16
-CUTS = 2
+CUTS = 4
 PUT = 8
 
 

time: 10.4 us -> 10.4 us (level)
  no operation moved by 1% of the time
where the time goes in v5:
time: 10.4 us; the launch traced here: 10.2 us
  Pallas kernels  9.6 us (92%)
  between operations  0.64 us (6%)
    pallas_call x1, Pallas kernels, local(): pl.pallas_call(functools.partial(kernel, (n_ex, n_col, n_lay, per_col, k_...  8.93 us
    pallas_call x1, Pallas kernels, local(): pl.pallas_call(put_out, out_shape=(jax.ShapeDtypeStruct(sketch.shape, ske...  0.67 us

profile of v5, /device:TPU:0, one launch (start us, length us, event | category | flops | bytes accessed | tf_op | source)
XLA Modules:
  0.0 10.2 jit_solution(3694623496058521115)
XLA Ops:
  0.6 8.9 %shard_map.77 = (bf16[32,2048]{1,0:T(8,128)(2,1)S(1)}, f32[1,32]{1,0:T(1,128)S(1)}) custom-call(bf16[64,4,896]{2,1,0:T(4,128)(2,1)} %bitcast.5, bf16[64,4,896]{2,1,0:T(4,128)(2,1)} %bitcast.6, s32[1,64]{1,0:T(1,128)} %order_hbm.1, s32[2,4,7]{2,1,0:T(4,128)} %bitcast.7, bf16[2,4,7]{2,1,0:T(4,128)(2,1)} %bitcast.8, bf16[1,2048]{1,0:T(2,128)(2,1)} %query_hbm.1), custom_call_target="tpu_custom_call" | custom-call | tf_op jit(solution)/shard_map/pallas_call | solution.py:625
  9.6 0.7 %shard_map.78 = (bf16[32,2048]{1,0:T(8,128)(2,1)}, f32[1,32]{1,0:T(1,128)}) custom-call(bf16[32,2048]{1,0:T(8,128)(2,1)S(1)} %get-tuple-element.6.sketch_ref, f32[1,32]{1,0:T(1,128)S(1)} %get-tuple-element.7.scores_ref), custom_call_target="tpu_custom_call" | custom-call | tf_op jit(solution)/shard_map/pallas_call | solution.py:673
